TPU v7x, 32 devices: a whole 2x2x4 slice. The times are simulated.
32 devices in a mesh: groups: 1, lat: 16 (over z, y, x), lon: 2 (over core).
Axes of the slice: x: 2, y: 2, z: 4, core: 2. Of those that a mesh axis runs over, the one named last changes fastest.
Arguments:
- fields: bfloat16 [64, 128, 256], P('groups', 'lat', 'lon'), may hold values from -6 to 6
- conv_first: bfloat16 [64, 64, 3, 3], replicated, may hold values from -0.25 to 0.25
- conv_second: bfloat16 [64, 64, 3, 3], replicated, may hold values from -0.25 to 0.25
- mixing: bfloat16 [64, 64, 64], P(None, 'lon'), may hold values from -0.75 to 0.75
Outputs:
- result: bfloat16 [64, 128, 256], P(('groups', 'lon'), 'lat')
All inputs are finite; a program needn't handle non-finite values.
Results may differ from a plain program's by a relative error of at most 0.0095.
Values may be sent and summed in bfloat16 or wider, within the bound.
A program may use at most 64 MiB of HBM per device.

v0:
```python
import math

import jax
import jax.numpy as jnp
from jax import lax
from jax.sharding import PartitionSpec as P


def padded_2(block, sides, width, periodic):
    for axis, dim in sides:
        count = lax.axis_size(axis)
        forward = [(i, i + 1) for i in range(count - 1)]
        if periodic:
            forward.append((count - 1, 0))
        backward = [(target, source) for source, target in forward]
        low = lax.ppermute(
            lax.slice_in_dim(block, block.shape[dim] - width, None, axis=dim), axis, forward
        )
        high = lax.ppermute(lax.slice_in_dim(block, 0, width, axis=dim), axis, backward)
        block = jnp.concatenate([low, block, high], axis=dim)
    return block


def forward_table(lon_total, orders):
    points = jnp.arange(lon_total, dtype=jnp.int32)[:, None]
    waves = jnp.arange(orders, dtype=jnp.int32)[None, :]
    angle = (points * waves % lon_total).astype(jnp.float32) * (2.0 * math.pi / lon_total)
    stacked = jnp.stack([jnp.cos(angle), -jnp.sin(angle)], axis=-1)
    return stacked.reshape(lon_total, 2 * orders).astype(jnp.bfloat16)


def inverse_table(lon_total, orders):
    waves = jnp.arange(orders, dtype=jnp.int32)[:, None]
    points = jnp.arange(lon_total, dtype=jnp.int32)[None, :]
    angle = (points * waves % lon_total).astype(jnp.float32) * (2.0 * math.pi / lon_total)
    factor = jnp.where(waves == 0, 1.0, 2.0).astype(jnp.float32)
    stacked = jnp.stack([factor * jnp.cos(angle), -factor * jnp.sin(angle)], axis=1)
    return stacked.reshape(2 * orders, lon_total).astype(jnp.bfloat16)


def quadrature(lat_total, lon_total):
    lat_rows = jnp.arange(lat_total, dtype=jnp.int32).astype(jnp.float32)
    colatitude = (lat_rows + 0.5) * (math.pi / lat_total)
    return jnp.sin(colatitude) * (math.pi / lat_total / lon_total)


def legendre_table(order_ids, degrees, lat_total):
    half_rows = lat_total // 2
    lat_rows = jnp.arange(half_rows, dtype=jnp.int32).astype(jnp.float32)
    colatitude = (lat_rows + 0.5) * (math.pi / lat_total)
    cosine = jnp.cos(colatitude)[None, :]
    sine_theta = jnp.sin(colatitude)[None, :]
    orders = order_ids.astype(jnp.float32)[:, None]
    counter = jnp.arange(1, degrees + 1, dtype=jnp.int32).astype(jnp.float32)
    log_terms = jnp.log((2.0 * counter - 1.0) / (2.0 * counter))
    below = counter[None, :] <= orders
    log_start = 0.5 * jnp.log(orders + 0.5) + 0.5 * jnp.sum(
        jnp.where(below, log_terms[None, :], 0.0), axis=1, keepdims=True
    )
    log_start = log_start + orders * jnp.log(sine_theta)
    block_span = 32

    def advance(carry, block_index):
        current, previous, log_scale = carry
        emitted = []
        for offset in range(block_span):
            degree = (block_index * block_span + offset).astype(jnp.float32)
            earlier = degree - 1.0
            coef_a = jnp.sqrt(
                jnp.maximum(4.0 * degree * degree - 1.0, 1.0)
                / jnp.maximum(degree * degree - orders * orders, 1.0)
            )
            coef_b = jnp.sqrt(
                jnp.maximum(earlier * earlier - orders * orders, 0.0)
                / jnp.maximum(4.0 * earlier * earlier - 1.0, 1.0)
            )
            newest = coef_a * (cosine * current - coef_b * previous)
            is_start = degree == orders
            before = degree < orders
            newest = jnp.where(before, 0.0, jnp.where(is_start, 1.0, newest))
            log_scale = jnp.where(is_start, log_start, log_scale)
            previous = jnp.where(is_start | before, 0.0, current)
            current = newest
            emitted.append(newest * jnp.exp(log_scale))
        size_now = jnp.maximum(jnp.abs(current), jnp.abs(previous))
        safe_size = jnp.where(size_now > 0.0, size_now, 1.0)
        carry_out = (current / safe_size, previous / safe_size, log_scale + jnp.log(safe_size))
        return (carry_out, jnp.stack(emitted, axis=-1))

    zeros = jnp.zeros((order_ids.shape[0], half_rows), jnp.float32)
    blocks = jnp.arange(degrees // block_span, dtype=jnp.int32)
    unused, stacked = lax.scan(advance, (zeros, zeros, zeros), blocks)
    northern = jnp.transpose(stacked, (1, 2, 0, 3)).reshape(order_ids.shape[0], half_rows, degrees)
    degree_ids = jnp.arange(degrees, dtype=jnp.int32)
    parity = (1 - 2 * ((degree_ids[None, :] + order_ids[:, None]) % 2)).astype(jnp.float32)
    southern = northern[:, ::-1, :] * parity[:, None, :]
    return jnp.concatenate([northern, southern], axis=1).astype(jnp.bfloat16)


def convolve(padded, kernel):
    return lax.conv_general_dilated(
        padded[None],
        kernel,
        (1, 1),
        "VALID",
        dimension_numbers=("NCHW", "OIHW", "NCHW"),
        preferred_element_type=jnp.float32,
    )[0]


def conv_layer(values, kernel):
    rimmed = padded_2(values, (("lat", 1),), 1, False)
    wrapped = padded_2(rimmed, (("lon", 2),), 1, True)
    return jnp.maximum(convolve(wrapped, kernel), 0.0).astype(jnp.bfloat16)


def local(fields, conv_first, conv_second, mixing):
    lat_count = lax.axis_size("lat")
    lon_count = lax.axis_size("lon")
    row_count = fields.shape[1]
    lat_total = row_count * lat_count
    lon_total = fields.shape[2] * lon_count
    orders = lat_total // 2
    degrees = mixing.shape[0]
    per_device = orders // lat_count
    lat_index = lax.axis_index("lat")
    hidden = conv_layer(conv_layer(fields, conv_first), conv_second)
    dft_table = forward_table(lon_total, orders)
    regrouped = lax.all_to_all(hidden, "lon", split_axis=0, concat_axis=2, tiled=True)
    spectra = jnp.dot(
        regrouped.reshape(-1, lon_total), dft_table, preferred_element_type=jnp.float32
    )
    spectra = spectra.reshape(regrouped.shape[0], row_count, 2 * orders)
    row_weights = lax.dynamic_slice_in_dim(
        quadrature(lat_total, lon_total), lat_index * row_count, row_count, 0
    )
    coeffs = (spectra * row_weights[None, :, None]).astype(jnp.bfloat16)
    order_ids = lat_index * per_device + jnp.arange(per_device, dtype=jnp.int32)
    legendre = legendre_table(order_ids, degrees, lat_total)
    item_block = lax.all_to_all(coeffs, "lat", split_axis=2, concat_axis=1, tiled=True)
    pieces = item_block.reshape(item_block.shape[0], lat_total, per_device, 2)
    spectral = jnp.einsum("cjmr,mjl->lcmr", pieces, legendre, preferred_element_type=jnp.float32)
    spectral = spectral.astype(jnp.bfloat16).reshape(degrees, item_block.shape[0], 2 * per_device)
    gathered = lax.all_gather(spectral, "lon", axis=1, tiled=True)
    mixed_coef = jnp.einsum(
        "lcx,loc->lox", gathered, mixing, preferred_element_type=jnp.float32
    ).astype(jnp.bfloat16)
    out_channels = mixed_coef.shape[1]
    mixed_pieces = mixed_coef.reshape(degrees, out_channels, per_device, 2)
    synthesis = jnp.einsum(
        "lomr,mjl->ojmr", mixed_pieces, legendre, preferred_element_type=jnp.float32
    )
    synthesis = synthesis.astype(jnp.bfloat16).reshape(out_channels, lat_total, 2 * per_device)
    back_table = inverse_table(lon_total, orders)
    item_block = lax.all_to_all(synthesis, "lat", split_axis=1, concat_axis=2, tiled=True)
    product = jnp.dot(
        item_block.reshape(-1, 2 * orders), back_table, preferred_element_type=jnp.float32
    )
    return product.reshape(item_block.shape[0], row_count, lon_total).astype(jnp.bfloat16)


def solution(mesh):
    in_specs = (P("groups", "lat", "lon"), P(), P(), P(None, "lon", None))
    out_specs = P(("groups", "lon"), "lat", None)
    return jax.shard_map(local, mesh=mesh, in_specs=in_specs, out_specs=out_specs, check_vma=False)
```

profile of v0, /device:TPU:0, one launch (start us, length us, event | category | flops | bytes accessed | tf_op | source)
XLA Modules:
  0.0 80.1 jit_solution(9734672846849882325)
XLA Ops:
  0.0 1.1 %fusion.139 = (bf16[64,1,128]{2,1,0:T(2,128)(2,1)S(1)}, bf16[64,1,128]{2,1,0:T(2,128)(2,1)S(1)}) fusion(bf16[64,8,128]{2,1,0:T(8,128)(2,1)} %param.6), kind=kLoop, calls=%fused_computation.367 | loop fusion | bytes 65536 | tf_op jit(solution)/shard_map/slice | solution.py:17
  1.1 4.8 %collective-permute-start = (bf16[64,1,128]{2,1,0:T(2,128)(2,1)S(1)}, bf16[64,1,128]{2,1,0:T(2,128)(2,1)S(1)}, u32[]{:S(2)}, u32[]{:S(2)}) collective-permute-start(bf16[64,1,128]{2,1,0:T(2,128)(2,1)S(1)} %get-tuple-element.867), channel_id=1, source_target_pairs={{0,2},{2,4},{4,6},{6,8},{8,10},{10,12},{12,14},{14,16},{16,18},{18... | collective-permute-start | bytes 49160 | tf_op jit(solution)/shard_map/ppermute | solution.py:16
  5.9 1.3 %collective-permute-start.1 = (bf16[64,1,128]{2,1,0:T(2,128)(2,1)S(1)}, bf16[64,1,128]{2,1,0:T(2,128)(2,1)S(1)}, u32[]{:S(2)}, u32[]{:S(2)}) collective-permute-start(bf16[64,1,128]{2,1,0:T(2,128)(2,1)S(1)} %get-tuple-element.868), channel_id=1, source_target_pairs={{2,0},{4,2},{6,4},{8,6},{10,8},{12,10},{14,12},{16,14},{18,16},{20... | collective-permute-start | bytes 49160 | tf_op jit(solution)/shard_map/ppermute | solution.py:19
  7.6 11.8 %while.23 = (s32[]{:T(128)}, f32[4,64]{1,0:T(4,128)S(1)}, f32[4,64]{1,0:T(4,128)S(1)}, f32[4,64]{1,0:T(4,128)S(1)}, f32[2,4,64,32]{2,1,3,0:T(4,128)S(1)}, /*inde...) while((s32[]{:T(128)}, f32[4,64]{1,0:T(4,128)S(1)}, ...), condition=%wide.region_2.3_spmd.clone.clone.clone.clone, body=%wide.region_1.2_spmd.clone.clone.clone.clone.sunk | while | flops 110306 | bytes 652777 | solution.py:92
  7.6 0.7 dynamic_slice.17
  13.5 0.7 dynamic_slice.17
  19.7 0.9 %copy-done.1 = bf16[64,8,128]{2,1,0:T(8,128)(2,1)S(1)} copy-done((bf16[64,8,128]{2,1,0:T(8,128)(2,1)S(1)}, bf16[64,8,128]{2,1,0:T(8,128)(2,1)}, u32[]{:S(2)}) %copy-start.1) | copy-done | bytes 131096
  21.7 0.7 collective-permute-done.2
  24.2 0.8 %copy-done.2 = bf16[64,64,3,3]{1,0,3,2:T(8,128)(2,1)S(1)} copy-done((bf16[64,64,3,3]{1,0,3,2:T(8,128)(2,1)S(1)}, bf16[64,64,3,3]{1,0,3,2:T(8,128)(2,1)}, u32[]{:S(2)}) %copy-start.2) | copy-done | bytes 73752
  25.0 0.8 %fusion.46 = bf16[8,8,17,64]{3,1,2,0:T(8,128)(2,1)S(1)} fusion(bf16[64,64,3,3]{1,0,3,2:T(8,128)(2,1)S(1)} %copy-done.2, bf16[64,10,1,7,2]{0,3,4,1,2:T(8,128)(2,1)S(1)} %slice.38, bf16[64,10,1,8,17]{0,3,4,1,2:T(8,128)(2,1)S(1)} %copy.134, pred[8,17]{0,1:T(8,128)(4,1)S(1)} %copy-done.4), kind=kOutput, calls=%fused_computation.245 | convolution fusion | flops 81008640 | bytes 405128 | tf_op jit(solution)/shard_map/conv_general_dilated | solution.py:101
  26.0 4.5 %collective-permute-start.4 = (bf16[64,1,128]{0,1,2:T(2,128)(2,1)S(1)}, bf16[64,1,128]{0,1,2:T(2,128)(2,1)S(1)}, u32[]{:S(2)}, u32[]{:S(2)}) collective-permute-start(bf16[64,1,128]{0,1,2:T(2,128)(2,1)S(1)} %get-tuple-element.861), channel_id=1, source_target_pairs={{0,2},{2,4},{4,6},{6,8},{8,10},{10,12},{12,14},{14,16},{16,18},{18... | collective-permute-start | bytes 49160 | tf_op jit(solution)/shard_map/ppermute | solution.py:16
  30.5 1.3 %collective-permute-start.5 = (bf16[64,1,128]{0,1,2:T(2,128)(2,1)S(1)}, bf16[64,1,128]{0,1,2:T(2,128)(2,1)S(1)}, u32[]{:S(2)}, u32[]{:S(2)}) collective-permute-start(bf16[64,1,128]{0,1,2:T(2,128)(2,1)S(1)} %get-tuple-element.862), channel_id=1, source_target_pairs={{2,0},{4,2},{6,4},{8,6},{10,8},{12,10},{14,12},{16,14},{18,16},{20... | collective-permute-start | bytes 49160 | tf_op jit(solution)/shard_map/ppermute | solution.py:19
  32.5 4.6 %collective-permute-done.5 = bf16[64,1,128]{0,1,2:T(2,128)(2,1)S(1)} collective-permute-done((bf16[64,1,128]{0,1,2:T(2,128)(2,1)S(1)}, bf16[64,1,128]{0,1,2:T(2,128)(2,1)S(1)}, u32[]{:S(2)}, u32[]{:S(2)}) %collective-permute-start.5) | collective-permute-done | bytes 16416 | tf_op jit(solution)/shard_map/ppermute | solution.py:19
  39.8 0.8 %copy-done.3 = bf16[64,64,3,3]{1,0,3,2:T(8,128)(2,1)S(1)} copy-done((bf16[64,64,3,3]{1,0,3,2:T(8,128)(2,1)S(1)}, bf16[64,64,3,3]{1,0,3,2:T(8,128)(2,1)}, u32[]{:S(2)}) %copy-start.3) | copy-done | bytes 73752
  40.6 0.8 %fusion.47 = bf16[8,8,17,64]{3,1,2,0:T(8,128)(2,1)S(1)} fusion(bf16[64,64,3,3]{1,0,3,2:T(8,128)(2,1)S(1)} %copy-done.3, bf16[64,10,1,7,2]{0,3,4,1,2:T(8,128)(2,1)S(1)} %slice.44, bf16[64,10,1,8,17]{0,3,4,1,2:T(8,128)(2,1)S(1)} %copy.141, pred[8,17]{0,1:T(8,128)(4,1)S(1)} %copy-done.4), kind=kOutput, calls=%fused_computation.246 | convolution fusion | flops 81008640 | bytes 405128 | tf_op jit(solution)/shard_map/conv_general_dilated | solution.py:101
  41.8 3.8 %all_to_all.45 = bf16[64,8,128]{2,1,0:T(8,128)(2,1)S(1)} all-to-all(bf16[64,8,128]{2,1,0:T(8,128)(2,1)S(1)} %copy.143), channel_id=1, replica_groups=mesh['groups'=1,'lat'=16,'lon'=2] {'lon'}, dimensions={0} | all-to-all | bytes 262144 | tf_op jit(solution)/shard_map/all_to_all | solution.py:129
  46.0 0.9 %reshape.2414 = bf16[16,2,1024]{2,1,0:T(2,128)(2,1)} reshape(bf16[128,8,32]{2,1,0:T(8,128)(2,1)S(1)} %bitcast.697) | data formatting | bytes 131072
  46.9 9.1 %all-to-all-start.1 = ((bf16[16,2,1024]{2,1,0:T(2,128)(2,1)}), bf16[16,2,1024]{2,1,0:T(2,128)(2,1)S(1)}, u32[]{:S(2)}, u32[]{:S(2)}) async-start(bf16[16,2,1024]{2,1,0:T(2,128)(2,1)} %reshape.2414), calls=%async_computation.1 | async-start | bytes 131072 | tf_op jit(solution)/shard_map/all_to_all | solution.py:140
  56.0 7.5 %all-to-all-done.1 = bf16[16,2,1024]{2,1,0:T(2,128)(2,1)S(1)} async-done(((bf16[16,2,1024]{2,1,0:T(2,128)(2,1)}), bf16[16,2,1024]{2,1,0:T(2,128)(2,1)S(1)}, u32[]{:S(2)}, u32[]{:S(2)}) %all-to-all-start.1) | async-done | bytes 65568 | tf_op jit(solution)/shard_map/all_to_all | solution.py:140
  64.1 1.9 %all_gather.3 = bf16[64,64,8]{0,2,1:T(8,128)(2,1)S(1)} all-gather(bf16[64,32,8]{0,2,1:T(8,128)(2,1)S(1)} %copy.151), channel_id=1, replica_groups=mesh['groups'=1,'lat'=16,'lon'=2] {'lon'}, dimensions={1}, use_global_device_ids=true | all-gather | bytes 98304 | tf_op jit(solution)/shard_map/all_gather | solution.py:144
  67.0 0.9 %reshape.2416 = bf16[16,2,1024]{2,1,0:T(2,128)(2,1)} reshape(bf16[128,8,32]{2,1,0:T(8,128)(2,1)S(1)} %bitcast.698) | data formatting | bytes 131072
  67.9 3.5 %all-to-all-start.2 = ((bf16[16,2,1024]{2,1,0:T(2,128)(2,1)}), bf16[16,2,1024]{2,1,0:T(2,128)(2,1)S(1)}, u32[]{:S(2)}, u32[]{:S(2)}) async-start(bf16[16,2,1024]{2,1,0:T(2,128)(2,1)} %reshape.2416), calls=%async_computation.2 | async-start | bytes 131072 | tf_op jit(solution)/shard_map/all_to_all | solution.py:155
  71.8 7.1 %all-to-all-done.2 = bf16[16,2,1024]{2,1,0:T(2,128)(2,1)S(1)} async-done(((bf16[16,2,1024]{2,1,0:T(2,128)(2,1)}), bf16[16,2,1024]{2,1,0:T(2,128)(2,1)S(1)}, u32[]{:S(2)}, u32[]{:S(2)}) %all-to-all-start.2) | async-done | bytes 65568 | tf_op jit(solution)/shard_map/all_to_all | solution.py:155
  79.3 0.8 %convolution_convert_fusion.1 = bf16[32,8,256]{2,1,0:T(8,128)(2,1)} fusion(bf16[32,8,128]{2,1,0:T(8,128)(2,1)S(1)} %copy.157, bf16[128,256,1]{1,0,2:T(8,128)(2,1)S(1)} %reshape.2412), kind=kOutput, calls=%fused_computation.248 | convolution fusion | flops 16842752 | bytes 262144 | tf_op jit(solution)/shard_map/dot_general | solution.py:156
  (249 shorter events, 17.3 us)
Async XLA Ops:
  0.0 66.1 %copy-start = (bf16[64,32,64]{2,1,0:T(8,128)(2,1)S(1)}, bf16[64,32,64]{2,1,0:T(8,128)(2,1)}, u32[]{:S(2)}) copy-start(bf16[64,32,64]{2,1,0:T(8,128)(2,1)} %param.9) | copy-start | bytes 786436
  1.1 18.6 %collective-permute-start = (bf16[64,1,128]{2,1,0:T(2,128)(2,1)S(1)}, bf16[64,1,128]{2,1,0:T(2,128)(2,1)S(1)}, u32[]{:S(2)}, u32[]{:S(2)}) collective-permute-start(bf16[64,1,128]{2,1,0:T(2,128)(2,1)S(1)} %get-tuple-element.867), channel_id=1, source_target_pairs={{0,2},{2,4},{4,6},{6,8},{8,10},{10,12},{12,14},{14,16},{16,18},{18... | collective-permute-start | bytes 49160 | tf_op jit(solution)/shard_map/ppermute | solution.py:16
  5.9 13.8 %collective-permute-start.1 = (bf16[64,1,128]{2,1,0:T(2,128)(2,1)S(1)}, bf16[64,1,128]{2,1,0:T(2,128)(2,1)S(1)}, u32[]{:S(2)}, u32[]{:S(2)}) collective-permute-start(bf16[64,1,128]{2,1,0:T(2,128)(2,1)S(1)} %get-tuple-element.868), channel_id=1, source_target_pairs={{2,0},{4,2},{6,4},{8,6},{10,8},{12,10},{14,12},{16,14},{18,16},{20... | collective-permute-start | bytes 49160 | tf_op jit(solution)/shard_map/ppermute | solution.py:19
  19.6 0.9 %copy-start.1 = (bf16[64,8,128]{2,1,0:T(8,128)(2,1)S(1)}, bf16[64,8,128]{2,1,0:T(8,128)(2,1)}, u32[]{:S(2)}) copy-start(bf16[64,8,128]{2,1,0:T(8,128)(2,1)} %param.6) | copy-start | bytes 393220
  20.9 1.6 %collective-permute-start.2 = (bf16[64,10,1]{2,1,0:T(8,128)(2,1)S(1)}, bf16[64,10,1]{2,1,0:T(8,128)(2,1)S(1)}, u32[]{:S(2)}, u32[]{:S(2)}) collective-permute-start(bf16[64,10,1]{2,1,0:T(8,128)(2,1)S(1)} %get-tuple-element.863), channel_id=1, source_target_pairs={{0,1},{1,0},{2,3},{3,2},{4,5},{5,4},{6,7},{7,6},{8,9},{9,8},{10,11... | collective-permute-start | bytes 3848 | tf_op jit(solution)/shard_map/ppermute | solution.py:16
  20.9 1.9 %collective-permute-start.3 = (bf16[64,10,1]{2,1,0:T(8,128)(2,1)S(1)}, bf16[64,10,1]{2,1,0:T(8,128)(2,1)S(1)}, u32[]{:S(2)}, u32[]{:S(2)}) collective-permute-start(bf16[64,10,1]{2,1,0:T(8,128)(2,1)S(1)} %get-tuple-element.864), channel_id=1, source_target_pairs={{1,0},{0,1},{3,2},{2,3},{5,4},{4,5},{7,6},{6,7},{9,8},{8,9},{11,10... | collective-permute-start | bytes 3848 | tf_op jit(solution)/shard_map/ppermute | solution.py:19
  24.1 0.9 %copy-start.2 = (bf16[64,64,3,3]{1,0,3,2:T(8,128)(2,1)S(1)}, bf16[64,64,3,3]{1,0,3,2:T(8,128)(2,1)}, u32[]{:S(2)}) copy-start(bf16[64,64,3,3]{1,0,3,2:T(8,128)(2,1)} %param.7) | copy-start | bytes 221188
  24.1 0.8 %copy-start.4 = (pred[8,17]{0,1:T(8,128)(4,1)S(1)}, pred[8,17]{0,1:T(8,128)(4,1)}, u32[]{:S(2)}) copy-start(pred[8,17]{0,1:T(8,128)(4,1)} %constant.444) | copy-start | bytes 412
  26.0 6.4 %collective-permute-start.4 = (bf16[64,1,128]{0,1,2:T(2,128)(2,1)S(1)}, bf16[64,1,128]{0,1,2:T(2,128)(2,1)S(1)}, u32[]{:S(2)}, u32[]{:S(2)}) collective-permute-start(bf16[64,1,128]{0,1,2:T(2,128)(2,1)S(1)} %get-tuple-element.861), channel_id=1, source_target_pairs={{0,2},{2,4},{4,6},{6,8},{8,10},{10,12},{12,14},{14,16},{16,18},{18... | collective-permute-start | bytes 49160 | tf_op jit(solution)/shard_map/ppermute | solution.py:16
  30.5 6.5 %collective-permute-start.5 = (bf16[64,1,128]{0,1,2:T(2,128)(2,1)S(1)}, bf16[64,1,128]{0,1,2:T(2,128)(2,1)S(1)}, u32[]{:S(2)}, u32[]{:S(2)}) collective-permute-start(bf16[64,1,128]{0,1,2:T(2,128)(2,1)S(1)} %get-tuple-element.862), channel_id=1, source_target_pairs={{2,0},{4,2},{6,4},{8,6},{10,8},{12,10},{14,12},{16,14},{18,16},{20... | collective-permute-start | bytes 49160 | tf_op jit(solution)/shard_map/ppermute | solution.py:19
  37.3 1.5 %collective-permute-start.6 = (bf16[64,10,1]{2,0,1:T(8,128)(2,1)S(1)}, bf16[64,10,1]{2,0,1:T(8,128)(2,1)S(1)}, u32[]{:S(2)}, u32[]{:S(2)}) collective-permute-start(bf16[64,10,1]{2,0,1:T(8,128)(2,1)S(1)} %get-tuple-element.865), channel_id=1, source_target_pairs={{0,1},{1,0},{2,3},{3,2},{4,5},{5,4},{6,7},{7,6},{8,9},{9,8},{10,11... | collective-permute-start | bytes 3848 | tf_op jit(solution)/shard_map/ppermute | solution.py:16
  37.4 1.6 %collective-permute-start.7 = (bf16[64,10,1]{2,0,1:T(8,128)(2,1)S(1)}, bf16[64,10,1]{2,0,1:T(8,128)(2,1)S(1)}, u32[]{:S(2)}, u32[]{:S(2)}) collective-permute-start(bf16[64,10,1]{2,0,1:T(8,128)(2,1)S(1)} %get-tuple-element.866), channel_id=1, source_target_pairs={{1,0},{0,1},{3,2},{2,3},{5,4},{4,5},{7,6},{6,7},{9,8},{8,9},{11,10... | collective-permute-start | bytes 3848 | tf_op jit(solution)/shard_map/ppermute | solution.py:19
  39.7 0.9 %copy-start.3 = (bf16[64,64,3,3]{1,0,3,2:T(8,128)(2,1)S(1)}, bf16[64,64,3,3]{1,0,3,2:T(8,128)(2,1)}, u32[]{:S(2)}) copy-start(bf16[64,64,3,3]{1,0,3,2:T(8,128)(2,1)} %param.8) | copy-start | bytes 221188
  46.9 16.6 %all-to-all-start.1 = ((bf16[16,2,1024]{2,1,0:T(2,128)(2,1)}), bf16[16,2,1024]{2,1,0:T(2,128)(2,1)S(1)}, u32[]{:S(2)}, u32[]{:S(2)}) async-start(bf16[16,2,1024]{2,1,0:T(2,128)(2,1)} %reshape.2414), calls=%async_computation.1 | async-start | bytes 131072 | tf_op jit(solution)/shard_map/all_to_all | solution.py:140
  67.9 11.0 %all-to-all-start.2 = ((bf16[16,2,1024]{2,1,0:T(2,128)(2,1)}), bf16[16,2,1024]{2,1,0:T(2,128)(2,1)S(1)}, u32[]{:S(2)}, u32[]{:S(2)}) async-start(bf16[16,2,1024]{2,1,0:T(2,128)(2,1)} %reshape.2416), calls=%async_computation.2 | async-start | bytes 131072 | tf_op jit(solution)/shard_map/all_to_all | solution.py:155
where the time goes:
time: 80.6 us; the launch traced here: 80.1 us
  starting transfers between devices  25.7 us (32%)
  waiting for transfers between devices  21.5 us (27%)
  local copies, waits for them, and re-layouts  10.6 us (13%)
  other arithmetic  9.55 us (12%)
  blocking collectives  5.74 us (7%)
  matrix products  3.51 us (4%)
  loops' own time  2.99 us (4%)
    ppermute x4, starting transfers between devices, padded_2(): lax.ppermute(lax.slice_in_dim(block, block.shape[dim] - width, None, axis...  9.54 us
    all_to_all x1, starting transfers between devices, local(): lax.all_to_all(coeffs, 'lat', split_axis=2, concat_axis=1, tiled=True)  9.07 us
    all_to_all x1, waiting for transfers between devices, local(): lax.all_to_all(coeffs, 'lat', split_axis=2, concat_axis=1, tiled=True)  7.51 us
    all_to_all x1, waiting for transfers between devices, local(): lax.all_to_all(synthesis, 'lat', split_axis=1, concat_axis=2, tiled=True)  7.08 us
    while x62, other arithmetic  5.6 us
    unnamed x16, local copies, waits for them, and re-layouts  5.39 us
    ppermute x4, waiting for transfers between devices, padded_2(): lax.ppermute(lax.slice_in_dim(block, 0, width, axis=dim), axis, backward)  5.17 us
    all_to_all x1, blocking collectives, local(): lax.all_to_all(hidden, 'lon', split_axis=0, concat_axis=2, tiled=True)  3.84 us
  transfers between devices with their start and end apart: 10, of which 8 were waited for; matrix products, arithmetic and copies ran while one was open for 13% of the time, Pallas kernels for 0%

commit v1 on v0

v1 whole, which is shorter than its diff:
```python
import functools
import math

import jax
import jax.numpy as jnp
import numpy as np
from jax import lax
from jax.experimental import pallas as pl
from jax.experimental.pallas import tpu as pltpu
from jax.sharding import PartitionSpec as P

MESH = pl.DeviceIdType.MESH
BF16 = jnp.bfloat16
F32 = jnp.float32


def mm(a, b, dims=((1,), (0,))):
    return lax.dot_general(a, b, (dims, ((), ())), preferred_element_type=F32)


def constant_tables(lat_count, rows, lon_total, orders, width, chans):
    lat_total = lat_count * rows
    per_x = 2 * orders // lat_count
    bf = jnp.bfloat16.dtype if hasattr(jnp.bfloat16, "dtype") else jnp.bfloat16
    k = np.arange(lon_total)[:, None]
    m = np.arange(orders)[None, :]
    angle = (k * m % lon_total).astype(np.float64) * (2.0 * math.pi / lon_total)
    forward = np.stack([np.cos(angle), -np.sin(angle)], axis=-1).reshape(lon_total, 2 * orders)
    factor = np.where(np.arange(orders) == 0, 1.0, 2.0)[:, None, None]
    inverse = np.stack([np.cos(angle.T), -np.sin(angle.T)], axis=1) * factor
    inverse = inverse.reshape(2 * orders, lon_total)
    forward = forward.T.reshape(lat_count, per_x, lon_total).transpose(1, 0, 2)
    forward = forward.reshape(2 * orders, lon_total)
    theta = (np.arange(lat_total) + 0.5) * (math.pi / lat_total)
    quad = np.sin(theta) * (math.pi / lat_total / lon_total)
    quad = np.broadcast_to(quad.reshape(lat_count, rows, 1), (lat_count, rows, width))
    half = lat_total // 2
    fold = np.concatenate([np.arange(half), np.arange(half)[::-1]])
    cosine = np.cos(theta[fold])[None, :]
    counter = np.arange(1, orders + 1)
    sums = np.concatenate([[0.0], np.cumsum(np.log((2.0 * counter - 1.0) / (2.0 * counter)))])
    ids = np.arange(orders)
    start = (0.5 * np.log(ids + 0.5) + 0.5 * sums[ids])[:, None] + ids[:, None] * np.log(np.sin(theta[fold]))[None, :]
    start = start.reshape(lat_count, per_x // 2, lat_total)
    pick = np.arange(lat_count)[:, None] == (np.arange(lat_total) // rows)[None, :]
    lane = np.arange(width) % chans
    squeeze = np.concatenate(
        [(lane[:, None] + h * chans) == np.arange(2 * chans)[None, :] for h in range(2)], axis=0
    )
    spread = lane[:, None] == lane[None, :]
    as_bf = lambda a: jnp.asarray(np.asarray(a, np.float32).astype(bf))
    as_f = lambda a: jnp.asarray(np.ascontiguousarray(a, np.float32))
    return (
        as_bf(forward), as_bf(inverse), as_f(quad), as_f(cosine), as_f(start),
        as_bf(pick), as_bf(squeeze), as_bf(spread),
    )


def body(sizes, x_ref, w1_ref, w2_ref, mix_ref, fwd_ref, inv_ref, quad_ref, cos_ref, start_ref,
         pick_ref, sq_ref, sp_ref, out_ref,
         xin, slab1, slab2, hdup, tb, send_b, recv_b, lt, lg, spec, tc, send_c, recv_c, mixed,
         a_send, a_recv, b_send, b_recv, c_send, c_recv):
    np_, rows, chans, half_w, degrees = sizes
    ch = chans // 2
    width = 2 * half_w
    per_x = 8
    orders_here = per_x // 2
    lat_total = np_ * rows
    lane_w = per_x * ch
    me = lax.axis_index("lat")
    core = lax.axis_index("lon")
    other = 1 - core

    barrier = pltpu.get_barrier_semaphore()

    def greet(d, _):
        p = lax.rem(me + d, np_)
        for h in range(2):
            pl.semaphore_signal(
                barrier, inc=1, device_id={"lat": p, "lon": (core + h) % 2}, device_id_type=MESH
            )
        return 0

    pl.semaphore_signal(barrier, inc=1, device_id={"lat": me, "lon": other}, device_id_type=MESH)
    lax.fori_loop(1, np_, greet, 0)

    cosine = cos_ref[...]
    log_start = start_ref[me]
    order = (me * orders_here + lax.broadcasted_iota(jnp.int32, (orders_here, lat_total), 0)).astype(F32)
    southern = lax.broadcasted_iota(jnp.int32, (orders_here, lat_total), 1) >= lat_total // 2
    order_odd = lax.broadcasted_iota(jnp.int32, (orders_here, lat_total), 0) + me * orders_here
    span = 32 if degrees % 32 == 0 else degrees

    def advance(block, carry):
        current, previous, log_scale = carry
        for offset in range(span):
            l_id = block * span + offset
            degree = l_id.astype(F32)
            earlier = degree - 1.0
            coef_a = jnp.sqrt(
                jnp.maximum(4.0 * degree * degree - 1.0, 1.0) / jnp.maximum(degree * degree - order * order, 1.0)
            )
            coef_b = jnp.sqrt(
                jnp.maximum(earlier * earlier - order * order, 0.0) / jnp.maximum(4.0 * earlier * earlier - 1.0, 1.0)
            )
            newest = coef_a * (cosine * current - coef_b * previous)
            is_start = order == degree
            before = order > degree
            newest = jnp.where(before, 0.0, jnp.where(is_start, 1.0, newest))
            log_scale = jnp.where(is_start, log_start, log_scale)
            previous = jnp.where(is_start | before, 0.0, current)
            current = newest
            value = newest * jnp.exp(log_scale)
            flip = southern & (((order_odd + l_id) & 1) == 1)
            value = jnp.where(flip, -value, value)
            for q in range(orders_here):
                lt[pl.ds(q * degrees + l_id, 1), :] = value[q : q + 1, :]
        size_now = jnp.maximum(jnp.abs(current), jnp.abs(previous))
        safe = jnp.where(size_now > 0.0, size_now, 1.0)
        return (current / safe, previous / safe, log_scale + jnp.log(safe))

    zeros = jnp.zeros((orders_here, lat_total), F32)
    lax.fori_loop(0, degrees // span, advance, (zeros, zeros, zeros))
    for q in range(orders_here):
        lg[q] = lt[q * degrees : (q + 1) * degrees, :].T.astype(BF16)

    pl.semaphore_wait(barrier, 2 * np_ - 1)

    def across():
        return pltpu.make_async_remote_copy(
            src_ref=x_ref, dst_ref=xin.at[core, pl.ds(2, rows)],
            send_sem=a_send.at[4], recv_sem=a_recv.at[4],
            device_id={"lat": me, "lon": other}, device_id_type=MESH,
        )

    def up(h):
        return pltpu.make_async_remote_copy(
            src_ref=x_ref.at[pl.ds(0, 2)], dst_ref=xin.at[core, pl.ds(rows + 2, 2)],
            send_sem=a_send.at[h], recv_sem=a_recv.at[h],
            device_id={"lat": jnp.maximum(me - 1, 0), "lon": (core + h) % 2}, device_id_type=MESH,
        )

    def down(h):
        return pltpu.make_async_remote_copy(
            src_ref=x_ref.at[pl.ds(rows - 2, 2)], dst_ref=xin.at[core, pl.ds(0, 2)],
            send_sem=a_send.at[2 + h], recv_sem=a_recv.at[2 + h],
            device_id={"lat": jnp.minimum(me + 1, np_ - 1), "lon": (core + h) % 2}, device_id_type=MESH,
        )

    @pl.when(me > 0)
    def _():
        up(0).start()
        up(1).start()

    @pl.when(me < np_ - 1)
    def _():
        down(0).start()
        down(1).start()

    across().start()

    @pl.when(me == 0)
    def _():
        xin[:, pl.ds(0, 2)] = jnp.zeros((2, 2, chans, half_w), BF16)

    @pl.when(me == np_ - 1)
    def _():
        xin[:, pl.ds(rows + 2, 2)] = jnp.zeros((2, 2, chans, half_w), BF16)

    xin[core, pl.ds(2, rows)] = x_ref[...]
    across().wait()

    def fill(slab, t, wide):
        base = t * 3 * chans
        slab[base : base + chans, :] = pltpu.roll(wide, 1, 1).astype(BF16)
        slab[base + chans : base + 2 * chans, :] = wide.astype(BF16)
        slab[base + 2 * chans : base + 3 * chans, :] = pltpu.roll(wide, width - 1, 1).astype(BF16)

    def row_in(t):
        return jnp.concatenate([xin[0, t].astype(F32), xin[1, t].astype(F32)], axis=1)

    for t in range(2, rows + 2):
        fill(slab1, t, row_in(t))

    @pl.when(me > 0)
    def _():
        up(0).wait_send()
        up(1).wait_send()
        down(0).wait_recv()
        down(1).wait_recv()

    @pl.when(me < np_ - 1)
    def _():
        down(0).wait_send()
        down(1).wait_send()
        up(0).wait_recv()
        up(1).wait_recv()

    for t in (0, 1, rows + 2, rows + 3):
        fill(slab1, t, row_in(t))

    w1 = w1_ref[...]
    w2 = w2_ref[core]
    depth = 9 * chans
    for t in range(rows + 2):
        first = mm(w1, slab1[t * 3 * chans : t * 3 * chans + depth, :])
        first = jnp.maximum(first, 0.0)
        if t == 0:
            first = jnp.where(me > 0, first, 0.0)
        if t == rows + 1:
            first = jnp.where(me < np_ - 1, first, 0.0)
        fill(slab2, t, first)

    dup = 128 // ch
    for t in range(rows):
        second = mm(w2, slab2[t * 3 * chans : t * 3 * chans + depth, :])
        second = jnp.maximum(second, 0.0).astype(BF16)
        for g in range(dup):
            hdup[t * 128 + g * ch : t * 128 + (g + 1) * ch, :] = second

    fwd = fwd_ref[...]
    group = lax.broadcasted_iota(jnp.int32, (np_, 128), 1) // ch
    for j in range(rows):
        s = mm(fwd, hdup[j * 128 : (j + 1) * 128, :], ((1,), (1,)))
        for xh in range(lane_w // 128):
            acc = s[xh * dup * np_ : (xh * dup + 1) * np_, :]
            for g in range(1, dup):
                at = (xh * dup + g) * np_
                acc = jnp.where(group == g, s[at : at + np_, :], acc)
            tb[xh, pl.ds(j, np_, stride=rows), :] = acc
    quad = quad_ref[me]
    for p in range(np_):
        piece = jnp.concatenate(
            [tb[xh, p * rows : (p + 1) * rows, :] for xh in range(lane_w // 128)], axis=1
        )
        send_b[p] = (piece * quad).astype(BF16)

    def b_copy(to_lat, to_core, from_lat, from_core):
        return pltpu.make_async_remote_copy(
            src_ref=send_b.at[to_lat], dst_ref=recv_b.at[from_core, from_lat],
            send_sem=b_send.at[to_core, to_lat], recv_sem=b_recv.at[from_core, from_lat],
            device_id={"lat": to_lat, "lon": to_core}, device_id_type=MESH,
        )

    def b_start(d, _):
        p = lax.rem(me + d, np_)
        for h in range(2):
            b_copy(p, (core + h) % 2, me, core).start()
        return 0

    lax.fori_loop(1, np_, b_start, 0)
    b_copy(me, other, me, core).start()
    recv_b[core, me] = send_b[me]

    def b_wait(d, _):
        q = lax.rem(me + np_ - d, np_)
        for h in range(2):
            b_copy(q, (core + h) % 2, q, (core + h) % 2).wait_recv()
        return 0

    b_copy(me, other, me, other).wait_recv()
    lax.fori_loop(1, np_, b_wait, 0)

    lt_b = lt[...].astype(BF16)
    x_lane = lax.broadcasted_iota(jnp.int32, (degrees, lane_w), 1) // ch
    halves = []
    for h in range(2):
        r = recv_b[h].astype(F32).reshape(lat_total, lane_w).astype(BF16)
        halves.append(mm(lt_b, r))
    for x in range(per_x):
        q = x // 2
        part = [jnp.where(x_lane == x, u[q * degrees : (q + 1) * degrees, :], 0.0).astype(BF16) for u in halves]
        spec[x * degrees : (x + 1) * degrees, :] = mm(jnp.concatenate(part, axis=1), sq_ref[...])

    sub = 8
    block = per_x * sub
    own = (
        lax.broadcasted_iota(jnp.int32, (block, sub * ch), 0) % sub
        == lax.broadcasted_iota(jnp.int32, (block, sub * ch), 1) // ch
    )
    for s in range(degrees // sub):
        lhs = jnp.concatenate(
            [spec[x * degrees + s * sub : x * degrees + (s + 1) * sub, :] for x in range(per_x)], axis=0
        ).astype(BF16)
        rhs = mix_ref[s * sub * ch : (s + 1) * sub * ch, :]
        both = jnp.where(own, mm(lhs, rhs, ((1,), (1,))), 0.0).astype(BF16)
        wide = mm(both, sp_ref[...])
        for x in range(per_x):
            mixed[x * degrees + s * sub : x * degrees + (s + 1) * sub, :] = wide[x * sub : (x + 1) * sub, :]

    own_row = (
        lax.broadcasted_iota(jnp.int32, (lat_total, lane_w), 0) % rows
        == lax.broadcasted_iota(jnp.int32, (lat_total, lane_w), 1) // ch
    )
    for x in range(per_x):
        y = mm(lg[x // 2], mixed[x * degrees : (x + 1) * degrees, :].astype(BF16))
        y = jnp.where(own_row, y, 0.0).astype(BF16)
        z = mm(pick_ref[...], y)
        for xh in range(lane_w // 128):
            tc[xh, pl.ds(x, np_, stride=per_x), :] = z[:, xh * 128 : (xh + 1) * 128]
    for p in range(np_):
        send_c[p] = jnp.concatenate(
            [tc[xh, p * per_x : (p + 1) * per_x, :] for xh in range(lane_w // 128)], axis=1
        ).astype(BF16)

    def c_copy(to_lat, from_lat):
        return pltpu.make_async_remote_copy(
            src_ref=send_c.at[to_lat], dst_ref=recv_c.at[from_lat],
            send_sem=c_send.at[to_lat], recv_sem=c_recv.at[from_lat],
            device_id={"lat": to_lat, "lon": core}, device_id_type=MESH,
        )

    def c_start(d, _):
        c_copy(lax.rem(me + d, np_), me).start()
        return 0

    lax.fori_loop(1, np_, c_start, 0)
    recv_c[me] = send_c[me]

    def b_done(d, _):
        p = lax.rem(me + d, np_)
        for h in range(2):
            b_copy(p, (core + h) % 2, me, core).wait_send()
        return 0

    b_copy(me, other, me, core).wait_send()
    lax.fori_loop(1, np_, b_done, 0)

    def c_wait(d, _):
        q = lax.rem(me + np_ - d, np_)
        c_copy(q, q).wait_recv()
        return 0

    lax.fori_loop(1, np_, c_wait, 0)
    full = recv_c[...].astype(F32).reshape(np_ * per_x, lane_w).T.astype(BF16)
    done = mm(full, inv_ref[...])
    for j in range(rows):
        out_ref[j] = done[j * ch : (j + 1) * ch, :].astype(BF16)

    def c_done(d, _):
        c_copy(lax.rem(me + d, np_), me).wait_send()
        return 0

    lax.fori_loop(1, np_, c_done, 0)


def local(np_, fields, conv_first, conv_second, mixing):
    chans, rows, half_w = fields.shape
    ch = chans // 2
    width = 2 * half_w
    lat_total = np_ * rows
    orders = lat_total // 2
    degrees = mixing.shape[0]
    per_x = 2 * orders // np_
    lane_w = per_x * ch
    tables = constant_tables(np_, rows, width, orders, lane_w, ch)
    x = jnp.transpose(fields, (1, 0, 2))
    w1 = jnp.transpose(conv_first, (0, 2, 3, 1)).reshape(chans, 9 * chans)
    w2 = jnp.transpose(conv_second, (0, 2, 3, 1)).reshape(2, ch, 9 * chans)
    mix = mixing.reshape(degrees * ch, chans)
    vm = pl.BlockSpec(memory_space=pltpu.VMEM)
    dma = pltpu.SemaphoreType.DMA
    out = pl.pallas_call(
        functools.partial(body, (np_, rows, chans, half_w, degrees)),
        out_shape=jax.ShapeDtypeStruct((rows, ch, width), BF16),
        in_specs=[vm] * 12,
        out_specs=vm,
        scratch_shapes=[
            pltpu.VMEM((2, rows + 4, chans, half_w), BF16),
            pltpu.VMEM(((rows + 4) * 3 * chans, width), BF16),
            pltpu.VMEM(((rows + 2) * 3 * chans, width), BF16),
            pltpu.VMEM((rows * 128, width), BF16),
            pltpu.VMEM((lane_w // 128, lat_total, 128), F32),
            pltpu.VMEM((np_, rows, lane_w), BF16),
            pltpu.VMEM((2, np_, rows, lane_w), BF16),
            pltpu.VMEM((per_x // 2 * degrees, lat_total), F32),
            pltpu.VMEM((per_x // 2, lat_total, degrees), BF16),
            pltpu.VMEM((per_x * degrees, chans), F32),
            pltpu.VMEM((lane_w // 128, np_ * per_x, 128), F32),
            pltpu.VMEM((np_, per_x, lane_w), BF16),
            pltpu.VMEM((np_, per_x, lane_w), BF16),
            pltpu.VMEM((per_x * degrees, lane_w), F32),
            dma((5,)), dma((5,)), dma((2, np_)), dma((2, np_)), dma((np_,)), dma((np_,)),
        ],
        compiler_params=pltpu.CompilerParams(
            collective_id=0, has_side_effects=True, vmem_limit_bytes=48 << 20
        ),
    )(x, w1, w2, mix, *tables)
    return jnp.transpose(out, (1, 0, 2))


def solution(mesh):
    in_specs = (P("groups", "lat", "lon"), P(), P(), P(None, "lon", None))
    out_specs = P(("groups", "lon"), "lat", None)
    return jax.shard_map(
        functools.partial(local, mesh.shape["lat"]),
        mesh=mesh, in_specs=in_specs, out_specs=out_specs, check_vma=False,
    )
```

time: 80.6 us -> 29.9 us (0.37)
  Pallas kernels: 0 us -> 26.4 us
  starting transfers between devices: 25.7 us -> 0 us
  waiting for transfers between devices: 21.5 us -> 0 us
  other arithmetic: 9.55 us -> 0 us
  local copies, waits for them, and re-layouts: 10.6 us -> 3.28 us
  blocking collectives: 5.74 us -> 0 us
  matrix products: 3.51 us -> 0 us
  loops' own time: 2.99 us -> 0 us
    pallas_call x0 -> x1, Pallas kernels: none -> 26.4 us  [local(): pl.pallas_call(functools.partial(body, (np_, rows, chans, half_w, degrees...]
    all_to_all x2 -> x0, waiting for transfers between devices: 14.6 us -> none  [the longest x1 7.51 us: local(): lax.all_to_all(coeffs, 'lat', split_axis=2, concat_axis=1, tiled=True)]
    ppermute x8 -> x0, starting transfers between devices: 13.1 us -> none  [the longest x4 9.54 us: padded_2(): lax.ppermute(lax.slice_in_dim(block, block.shape[dim] - width, None, axis...]
    all_to_all x2 -> x0, starting transfers between devices: 12.6 us -> none  [the longest x1 9.07 us: local(): lax.all_to_all(coeffs, 'lat', split_axis=2, concat_axis=1, tiled=True)]
    ppermute x8 -> x0, waiting for transfers between devices: 6.93 us -> none  [the longest x4 5.17 us: padded_2(): lax.ppermute(lax.slice_in_dim(block, 0, width, axis=dim), axis, backward)]
    while x62 -> x0, other arithmetic: 5.6 us -> none
    unnamed x16 -> x23, local copies, waits for them, and re-layouts: 5.39 us -> 1 us
    all_to_all x1 -> x0, blocking collectives: 3.84 us -> none  [local(): lax.all_to_all(hidden, 'lon', split_axis=0, concat_axis=2, tiled=True)]
  transfers between devices with their start and end apart: 10 -> 0, of which waited for: 8 -> 0; matrix products, arithmetic and copies ran while one was open for 13% -> 0% of each run, Pallas kernels for 0% -> 0%
where the time goes in v1:
time: 29.9 us; the launch traced here: 29.8 us
  Pallas kernels  26.4 us (88%)
  local copies, waits for them, and re-layouts  3.28 us (11%)
    pallas_call x1, Pallas kernels, local(): pl.pallas_call(functools.partial(body, (np_, rows, chans, half_w, degrees...  26.4 us
    transpose x1, local copies, waits for them, and re-layouts, local(): w2 = jnp.transpose(conv_second, (0, 2, 3, 1)).reshape(2, ch, 9 * chans)  1.08 us
    unnamed x23, local copies, waits for them, and re-layouts  1 us
    transpose x1, local copies, waits for them, and re-layouts, local(): return jnp.transpose(out, (1, 0, 2))  0.73 us

profile of v1, /device:TPU:0, one launch (start us, length us, event | category | flops | bytes accessed | tf_op | source)
XLA Modules:
  0.0 29.8 jit_solution(18402268749930792061)
XLA Ops:
  0.0 1.1 %copy.19 = bf16[64,3,3,64]{3,2,1,0:T(4,128)(2,1)S(1)} copy(bf16[64,3,3,64]{3,0,2,1:T(8,128)(2,1)} %bitcast.13) | data formatting | bytes 147456 | tf_op jit(solution)/shard_map/transpose | solution.py:359
  1.1 0.0 copy-start
  1.1 0.2 reshape.10.w2_ref
  1.3 0.0 copy-done.9
  1.3 0.0 copy-start.5
  1.3 0.2 copy.18
  1.5 0.0 copy-start.3
  1.5 0.0 copy-start.4
  1.5 0.0 copy-start.7
  1.5 0.1 copy.20.w1_ref
  1.6 0.0 copy-done.10
  1.6 0.0 copy-start.1
  1.7 0.0 copy-start.2
  1.7 0.0 copy-start.8
  1.7 0.0 copy-done.6
  1.7 0.4 %copy-done = bf16[64,32,64]{2,1,0:T(8,128)(2,1)S(1)} copy-done((bf16[64,32,64]{2,1,0:T(8,128)(2,1)S(1)}, bf16[64,32,64]{2,1,0:T(8,128)(2,1)}, u32[]{:S(2)}) %copy-start) | copy-done | bytes 262168
  2.1 0.0 copy-done.5
  2.2 0.3 copy-done.3
  2.4 0.0 copy-done.4
  2.4 0.0 copy-done.7
  2.4 0.2 copy-done.1
  2.6 0.0 copy-done.2
  2.7 26.4 %shard_map.118 = bf16[8,32,256]{2,1,0:T(8,128)(2,1)S(1)} custom-call(bf16[8,64,128]{2,1,0:T(8,128)(2,1)S(1)} %bitcast.10, bf16[64,576]{1,0:T(8,128)(2,1)S(1)} %copy.20.w1_ref, bf16[2,32,576]{2,1,0:T(8,128)(2,1)S(1)} %reshape.10.w2_ref, bf16[2048,64]{1,0:T(8,128)(2,1)S(1)} %bitcast.8, bf16[128,256]{1,0:T(8,128)(2,1)S(1)} %copy-done.4, ...), custom_call_target="tpu_custom_call" | custom-call | tf_op jit(solution)/shard_map/pallas_call | solution.py:363
  29.0 0.7 %copy.21 = bf16[32,8,256]{2,1,0:T(8,128)(2,1)} copy(bf16[32,8,256]{2,0,1:T(8,128)(2,1)S(1)} %bitcast.9) | data formatting | bytes 262144 | tf_op jit(solution)/shard_map/transpose | solution.py:389
  (5 shorter events, 0.0 us)
Async XLA Ops:
  0.0 1.3 %copy-start.9 = (bf16[64,64,3,3]{1,0,3,2:T(8,128)(2,1)S(1)}, bf16[64,64,3,3]{1,0,3,2:T(8,128)(2,1)}, u32[]{:S(2)}) copy-start(bf16[64,64,3,3]{1,0,3,2:T(8,128)(2,1)} %param.13) | copy-start | bytes 221188
  0.0 1.6 %copy-start.10 = (bf16[64,8,128]{2,1,0:T(8,128)(2,1)S(1)}, bf16[64,8,128]{2,1,0:T(8,128)(2,1)}, u32[]{:S(2)}) copy-start(bf16[64,8,128]{2,1,0:T(8,128)(2,1)} %param.12) | copy-start | bytes 393220
  0.0 1.7 %copy-start.6 = (f32[16,4,128]{2,1,0:T(4,128)S(1)}, f32[16,4,128]{2,1,0:T(4,128)}, u32[]{:S(2)}) copy-start(f32[16,4,128]{2,1,0:T(4,128)} %constant.20.clone.start_ref) | copy-start | bytes 98308
  1.1 1.0 %copy-start = (bf16[64,32,64]{2,1,0:T(8,128)(2,1)S(1)}, bf16[64,32,64]{2,1,0:T(8,128)(2,1)}, u32[]{:S(2)}) copy-start(bf16[64,32,64]{2,1,0:T(8,128)(2,1)} %param.15) | copy-start | bytes 786436
  1.3 0.9 %copy-start.5 = (bf16[128,256]{1,0:T(8,128)(2,1)S(1)}, bf16[128,256]{1,0:T(8,128)(2,1)}, u32[]{:S(2)}) copy-start(bf16[128,256]{1,0:T(8,128)(2,1)} %constant.17.clone.inv_ref) | copy-start | bytes 196612
  1.5 1.0 %copy-start.3 = (bf16[256,256]{1,0:T(8,128)(2,1)S(1)}, bf16[256,256]{1,0:T(8,128)(2,1)}, u32[]{:S(2)}) copy-start(bf16[256,256]{1,0:T(8,128)(2,1)} %constant.23.clone.sp_ref) | copy-start | bytes 393220
  1.5 0.9 %copy-start.4 = (bf16[128,256]{1,0:T(8,128)(2,1)S(1)}, bf16[128,256]{1,0:T(8,128)(2,1)}, u32[]{:S(2)}) copy-start(bf16[128,256]{1,0:T(8,128)(2,1)} %constant.16.clone.fwd_ref) | copy-start | bytes 196612
  1.5 0.9 %copy-start.7 = (bf16[16,128]{1,0:T(8,128)(2,1)S(1)}, bf16[16,128]{1,0:T(8,128)(2,1)}, u32[]{:S(2)}) copy-start(bf16[16,128]{1,0:T(8,128)(2,1)} %constant.21.clone.pick_ref) | copy-start | bytes 12292
  1.6 1.0 %copy-start.1 = (f32[16,8,256]{2,1,0:T(8,128)S(1)}, f32[16,8,256]{2,1,0:T(8,128)}, u32[]{:S(2)}) copy-start(f32[16,8,256]{2,1,0:T(8,128)} %constant.18.clone.quad_ref) | copy-start | bytes 393220
  1.7 1.0 %copy-start.2 = (bf16[512,64]{1,0:T(8,128)(2,1)S(1)}, bf16[512,64]{1,0:T(8,128)(2,1)}, u32[]{:S(2)}) copy-start(bf16[512,64]{1,0:T(8,128)(2,1)} %constant.22.clone.sq_ref) | copy-start | bytes 196612
  1.7 1.0 %copy-start.8 = (f32[1,128]{1,0:T(1,128)S(1)}, f32[1,128]{1,0:T(1,128)}, u32[]{:S(2)}) copy-start(f32[1,128]{1,0:T(1,128)} %constant.19.clone.cos_ref) | copy-start | bytes 1540

commit v2 on v1

v2 whole, which is shorter than its diff:
```python
import functools
import math

import jax
import jax.numpy as jnp
import numpy as np
from jax import lax
from jax.experimental import pallas as pl
from jax.experimental.pallas import tpu as pltpu
from jax.sharding import PartitionSpec as P

MESH = pl.DeviceIdType.MESH
BF16 = jnp.bfloat16
F32 = jnp.float32


def mm(a, b, dims=((1,), (0,))):
    return lax.dot_general(a, b, (dims, ((), ())), preferred_element_type=F32)


def constant_tables(lat_count, rows, lon_total, orders, width):
    lat_total = lat_count * rows
    per_x = 2 * orders // lat_count
    k = np.arange(lon_total)[:, None]
    m = np.arange(orders)[None, :]
    angle = (k * m % lon_total).astype(np.float64) * (2.0 * math.pi / lon_total)
    forward = np.stack([np.cos(angle), -np.sin(angle)], axis=-1).reshape(lon_total, 2 * orders)
    factor = np.where(np.arange(orders) == 0, 1.0, 2.0)[:, None, None]
    inverse = np.stack([np.cos(angle.T), -np.sin(angle.T)], axis=1) * factor
    inverse = inverse.reshape(2 * orders, lon_total)
    forward = forward.T.reshape(lat_count, per_x, lon_total).transpose(1, 0, 2)
    forward = forward.reshape(2 * orders, lon_total)
    theta = (np.arange(lat_total) + 0.5) * (math.pi / lat_total)
    quad = np.sin(theta) * (math.pi / lat_total / lon_total)
    quad = np.broadcast_to(quad.reshape(lat_count, rows, 1), (lat_count, rows, width))
    half = lat_total // 2
    fold = np.concatenate([np.arange(half), np.arange(half)[::-1]])
    cosine = np.cos(theta[fold])[None, :]
    counter = np.arange(1, orders + 1)
    sums = np.concatenate([[0.0], np.cumsum(np.log((2.0 * counter - 1.0) / (2.0 * counter)))])
    ids = np.arange(orders)
    start = (0.5 * np.log(ids + 0.5) + 0.5 * sums[ids])[:, None] + ids[:, None] * np.log(np.sin(theta[fold]))[None, :]
    start = start.reshape(lat_count, per_x // 2, lat_total)
    start = np.pad(start, ((0, 0), (0, 8 - per_x // 2), (0, 0)))
    as_bf = lambda a: jnp.asarray(np.asarray(a, np.float32).astype(jnp.bfloat16))
    as_f = lambda a: jnp.asarray(np.ascontiguousarray(a, np.float32))
    return as_bf(forward), as_bf(inverse), as_f(quad), as_f(cosine), as_f(start)


def peers(np_, me):
    if np_ & (np_ - 1):
        return [lax.rem(me + d, np_) for d in range(np_ - 1, 0, -1)]
    out = []
    for d in range(np_ - 1, 0, -1):
        p, bit = me, 1
        while bit < np_:
            if d & bit:
                p = p + bit - 2 * bit * (me // bit % 2)
            bit *= 2
        out.append(p)
    return out


def body(sizes, x_ref, w1_ref, w2_ref, cos_ref, mix_hbm, fwd_hbm, inv_hbm, quad_hbm, start_hbm, out_ref,
         xin, slab1, slab2, hdup, tb, send_b, recv_b, lt, lt_b, lg, spec, tc, send_c, recv_c, mixed,
         w1s, w2s, sq_s, sp_s, mix_s, fwd_s, inv_s, quad_s, start_s,
         a_send, a_recv, b_send, b_recv, c_send, c_recv, l_sem):
    np_, rows, chans, half_w, degrees = sizes
    ch = chans // 2
    width = 2 * half_w
    per_x = 8
    orders_here = per_x // 2
    lat_total = np_ * rows
    lane_w = per_x * ch
    me = lax.axis_index("lat")
    core = lax.axis_index("lon")
    other = 1 - core

    barrier = pltpu.get_barrier_semaphore()

    others = peers(np_, me)
    pl.semaphore_signal(barrier, inc=1, device_id={"lat": me, "lon": other}, device_id_type=MESH)
    for p in others:
        for h in (core, other):
            pl.semaphore_signal(barrier, inc=1, device_id={"lat": p, "lon": h}, device_id_type=MESH)

    loads = [
        pltpu.make_async_copy(a, b, l_sem.at[k])
        for k, (a, b) in enumerate([
            (start_hbm.at[me], start_s), (quad_hbm.at[me], quad_s), (fwd_hbm, fwd_s),
            (mix_hbm, mix_s), (inv_hbm, inv_s),
        ])
    ]
    for load in loads:
        load.start()

    for k in range(9):
        at = slice(k * chans, (k + 1) * chans)
        w1s[:, at] = w1_ref[k // 3, k % 3]
        w2s[:, at] = w2_ref[k // 3, k % 3, pl.ds(pl.multiple_of(core * ch, ch), ch), :]

    pl.semaphore_wait(barrier, 2 * np_ - 1)

    def across():
        return pltpu.make_async_remote_copy(
            src_ref=x_ref, dst_ref=xin.at[core, pl.ds(2, rows)],
            send_sem=a_send.at[4], recv_sem=a_recv.at[4],
            device_id={"lat": me, "lon": other}, device_id_type=MESH,
        )

    def up(h):
        return pltpu.make_async_remote_copy(
            src_ref=x_ref.at[pl.ds(0, 2)], dst_ref=xin.at[core, pl.ds(rows + 2, 2)],
            send_sem=a_send.at[h], recv_sem=a_recv.at[h],
            device_id={"lat": jnp.maximum(me - 1, 0), "lon": (core + h) % 2}, device_id_type=MESH,
        )

    def down(h):
        return pltpu.make_async_remote_copy(
            src_ref=x_ref.at[pl.ds(rows - 2, 2)], dst_ref=xin.at[core, pl.ds(0, 2)],
            send_sem=a_send.at[2 + h], recv_sem=a_recv.at[2 + h],
            device_id={"lat": jnp.minimum(me + 1, np_ - 1), "lon": (core + h) % 2}, device_id_type=MESH,
        )

    @pl.when(me > 0)
    def _():
        up(0).start()
        up(1).start()

    @pl.when(me < np_ - 1)
    def _():
        down(0).start()
        down(1).start()

    across().start()

    @pl.when(me == 0)
    def _():
        xin[:, pl.ds(0, 2)] = jnp.zeros((2, 2, chans, half_w), BF16)

    @pl.when(me == np_ - 1)
    def _():
        xin[:, pl.ds(rows + 2, 2)] = jnp.zeros((2, 2, chans, half_w), BF16)

    xin[core, pl.ds(2, rows)] = x_ref[...]

    loads[0].wait()
    cosine = cos_ref[...]
    log_start = start_s[...]
    wide_l = (8, degrees)
    order = (lax.broadcasted_iota(jnp.int32, wide_l, 0) + me * orders_here).astype(F32)
    degree = lax.broadcasted_iota(jnp.int32, wide_l, 1).astype(F32)
    earlier = degree - 1.0
    coef_a = jnp.sqrt(
        jnp.maximum(4.0 * degree * degree - 1.0, 1.0) / jnp.maximum(degree * degree - order * order, 1.0)
    )
    coef_b = coef_a * jnp.sqrt(
        jnp.maximum(earlier * earlier - order * order, 0.0) / jnp.maximum(4.0 * earlier * earlier - 1.0, 1.0)
    )
    wide_j = (8, lat_total)
    order_id = lax.broadcasted_iota(jnp.int32, wide_j, 0) + me * orders_here
    southern = lax.broadcasted_iota(jnp.int32, wide_j, 1) >= lat_total // 2
    sign_even = jnp.where(southern & (order_id % 2 == 1), -1.0, 1.0)
    sign_odd = jnp.where(southern & (order_id % 2 == 0), -1.0, 1.0)
    start_scale = jnp.exp(log_start)
    span = 32 if degrees % 32 == 0 else degrees
    current = previous = log_scale = scale = jnp.zeros(wide_j, F32)
    for l_id in range(degrees):
        is_start = order_id == l_id
        newest = (
            (coef_a[:, l_id : l_id + 1] * cosine) * current
            - coef_b[:, l_id : l_id + 1] * previous
            + jnp.where(is_start, 1.0, 0.0)
        )
        scale = jnp.where(is_start, start_scale, scale)
        previous, current = current, newest
        value = newest * (scale * (sign_odd if l_id % 2 else sign_even))
        for v in range(lat_total // 128):
            lt[v, l_id * 8 : (l_id + 1) * 8, :] = value[:, v * 128 : (v + 1) * 128]
        if (l_id + 1) % span == 0 and l_id + 1 < degrees:
            log_scale = jnp.where((order_id > l_id - span) & (order_id <= l_id), log_start, log_scale)
            size_now = jnp.maximum(jnp.abs(current), jnp.abs(previous))
            safe = jnp.where(size_now > 0.0, size_now, 1.0)
            current = current / safe
            previous = previous / safe
            log_scale = log_scale + jnp.log(safe)
            scale = jnp.exp(log_scale)
    across().wait()

    def fill(slab, t, wide):
        base = t * 3 * chans
        slab[base : base + chans, :] = pltpu.roll(wide, 1, 1).astype(BF16)
        slab[base + chans : base + 2 * chans, :] = wide.astype(BF16)
        slab[base + 2 * chans : base + 3 * chans, :] = pltpu.roll(wide, width - 1, 1).astype(BF16)

    def row_in(t):
        return jnp.concatenate([xin[0, t].astype(F32), xin[1, t].astype(F32)], axis=1)

    for t in range(2, rows + 2):
        fill(slab1, t, row_in(t))

    @pl.when(me > 0)
    def _():
        up(0).wait_send()
        up(1).wait_send()
        down(0).wait_recv()
        down(1).wait_recv()

    @pl.when(me < np_ - 1)
    def _():
        down(0).wait_send()
        down(1).wait_send()
        up(0).wait_recv()
        up(1).wait_recv()

    for t in (0, 1, rows + 2, rows + 3):
        fill(slab1, t, row_in(t))

    w1 = w1s[...]
    w2 = w2s[...]
    depth = 9 * chans
    for t in range(rows + 2):
        first = mm(w1, slab1[t * 3 * chans : t * 3 * chans + depth, :])
        first = jnp.maximum(first, 0.0)
        if t == 0:
            first = jnp.where(me > 0, first, 0.0)
        if t == rows + 1:
            first = jnp.where(me < np_ - 1, first, 0.0)
        fill(slab2, t, first)

    dup = 128 // ch
    for t in range(rows):
        second = mm(w2, slab2[t * 3 * chans : t * 3 * chans + depth, :])
        second = jnp.maximum(second, 0.0).astype(BF16)
        for g in range(dup):
            hdup[t * 128 + g * ch : t * 128 + (g + 1) * ch, :] = second

    loads[1].wait()
    loads[2].wait()
    fwd = fwd_s[...]
    group = lax.broadcasted_iota(jnp.int32, (np_, 128), 1) // ch
    for j in range(rows):
        s = mm(fwd, hdup[j * 128 : (j + 1) * 128, :], ((1,), (1,)))
        for xh in range(lane_w // 128):
            acc = s[xh * dup * np_ : (xh * dup + 1) * np_, :]
            for g in range(1, dup):
                at = (xh * dup + g) * np_
                acc = jnp.where(group == g, s[at : at + np_, :], acc)
            tb[xh, pl.ds(j, np_, stride=rows), :] = acc
    quad = quad_s[...]
    for p in range(np_):
        piece = jnp.concatenate(
            [tb[xh, p * rows : (p + 1) * rows, :] for xh in range(lane_w // 128)], axis=1
        )
        send_b[p] = (piece * quad).astype(BF16)

    def b_copy(to_lat, to_core, from_lat, from_core):
        return pltpu.make_async_remote_copy(
            src_ref=send_b.at[to_lat], dst_ref=recv_b.at[from_core, from_lat],
            send_sem=b_send.at[to_core, to_lat], recv_sem=b_recv.at[from_core, from_lat],
            device_id={"lat": to_lat, "lon": to_core}, device_id_type=MESH,
        )

    for p in others:
        for h in (core, other):
            b_copy(p, h, me, core).start()
    b_copy(me, other, me, core).start()
    recv_b[core, me] = send_b[me]

    for q in range(orders_here):
        table = jnp.concatenate(
            [lt[v, pl.ds(q, degrees, stride=8), :] for v in range(lat_total // 128)], axis=1
        )
        lt_b[q * degrees : (q + 1) * degrees, :] = table.astype(BF16)
        lg[q] = table.T.astype(BF16)
    at = lax.broadcasted_iota(jnp.int32, (2 * lane_w, chans), 0)
    place = at // lane_w * ch + at % ch
    sq_s[...] = jnp.where(
        place == lax.broadcasted_iota(jnp.int32, (2 * lane_w, chans), 1), 1.0, 0.0
    ).astype(BF16)
    sp_s[...] = jnp.where(
        lax.broadcasted_iota(jnp.int32, (lane_w, rows * ch), 0) % ch
        == lax.broadcasted_iota(jnp.int32, (lane_w, rows * ch), 1) // rows, 1.0, 0.0
    ).astype(BF16)
    pick = jnp.where(
        lax.broadcasted_iota(jnp.int32, (np_, lat_total), 0)
        == lax.broadcasted_iota(jnp.int32, (np_, lat_total), 1) // rows, 1.0, 0.0
    ).astype(BF16)
    loads[3].wait()
    loads[4].wait()

    b_copy(me, other, me, other).wait_recv()
    for q in reversed(others):
        for h in (core, other):
            b_copy(q, h, q, h).wait_recv()

    table = lt_b[...]
    x_lane = lax.broadcasted_iota(jnp.int32, (degrees, lane_w), 1) // ch
    halves = []
    for h in range(2):
        r = recv_b[h].astype(F32).reshape(lat_total, lane_w).astype(BF16)
        halves.append(mm(table, r))
    for x in range(per_x):
        q = x // 2
        part = [jnp.where(x_lane == x, u[q * degrees : (q + 1) * degrees, :], 0.0).astype(BF16) for u in halves]
        spec[x * degrees : (x + 1) * degrees, :] = mm(jnp.concatenate(part, axis=1), sq_s[...])

    sub = 8
    block = per_x * sub
    own = (
        lax.broadcasted_iota(jnp.int32, (block, sub * ch), 0) % sub
        == lax.broadcasted_iota(jnp.int32, (block, sub * ch), 1) // ch
    )
    for s in range(degrees // sub):
        lhs = jnp.concatenate(
            [spec[x * degrees + s * sub : x * degrees + (s + 1) * sub, :] for x in range(per_x)], axis=0
        ).astype(BF16)
        rhs = mix_s[s * sub * ch : (s + 1) * sub * ch, :]
        both = jnp.where(own, mm(lhs, rhs, ((1,), (1,))), 0.0).astype(BF16)
        wide = mm(both, sp_s[...])
        for x in range(per_x):
            mixed[x * degrees + s * sub : x * degrees + (s + 1) * sub, :] = wide[x * sub : (x + 1) * sub, :]

    own_row = (
        lax.broadcasted_iota(jnp.int32, (lat_total, lane_w), 0) % rows
        == lax.broadcasted_iota(jnp.int32, (lat_total, lane_w), 1) % rows
    )
    for x in range(per_x):
        y = mm(lg[x // 2], mixed[x * degrees : (x + 1) * degrees, :].astype(BF16))
        y = jnp.where(own_row, y, 0.0).astype(BF16)
        z = mm(pick, y)
        for xh in range(lane_w // 128):
            tc[xh, pl.ds(x, np_, stride=per_x), :] = z[:, xh * 128 : (xh + 1) * 128]
    for p in range(np_):
        send_c[p] = jnp.concatenate(
            [tc[xh, p * per_x : (p + 1) * per_x, :] for xh in range(lane_w // 128)], axis=1
        ).astype(BF16)

    def c_copy(to_lat, from_lat):
        return pltpu.make_async_remote_copy(
            src_ref=send_c.at[to_lat], dst_ref=recv_c.at[from_lat],
            send_sem=c_send.at[to_lat], recv_sem=c_recv.at[from_lat],
            device_id={"lat": to_lat, "lon": core}, device_id_type=MESH,
        )

    for p in others:
        c_copy(p, me).start()
    recv_c[me] = send_c[me]

    b_copy(me, other, me, core).wait_send()
    for p in others:
        for h in (core, other):
            b_copy(p, h, me, core).wait_send()

    for q in reversed(others):
        c_copy(q, q).wait_recv()
    full = recv_c[...].astype(F32).reshape(np_ * per_x, lane_w).T.astype(BF16)
    out_ref[...] = mm(full, inv_s[...]).astype(BF16)
    for p in others:
        c_copy(p, me).wait_send()


def local(np_, fields, conv_first, conv_second, mixing):
    chans, rows, half_w = fields.shape
    ch = chans // 2
    width = 2 * half_w
    lat_total = np_ * rows
    orders = lat_total // 2
    degrees = mixing.shape[0]
    per_x = 2 * orders // np_
    lane_w = per_x * ch
    forward, inverse, quad, cosine, start = constant_tables(np_, rows, width, orders, lane_w)
    x = jnp.transpose(fields, (1, 0, 2))
    w1 = jnp.transpose(conv_first, (2, 3, 0, 1))
    w2 = jnp.transpose(conv_second, (2, 3, 0, 1))
    mix = mixing.reshape(degrees * ch, chans)
    vm = pl.BlockSpec(memory_space=pltpu.VMEM)
    hbm = pl.BlockSpec(memory_space=pltpu.HBM)
    dma = pltpu.SemaphoreType.DMA
    out = pl.pallas_call(
        functools.partial(body, (np_, rows, chans, half_w, degrees)),
        out_shape=jax.ShapeDtypeStruct((ch * rows, width), BF16),
        in_specs=[vm] * 4 + [hbm] * 5,
        out_specs=vm,
        scratch_shapes=[
            pltpu.VMEM((2, rows + 4, chans, half_w), BF16),
            pltpu.VMEM(((rows + 4) * 3 * chans, width), BF16),
            pltpu.VMEM(((rows + 2) * 3 * chans, width), BF16),
            pltpu.VMEM((rows * 128, width), BF16),
            pltpu.VMEM((lane_w // 128, lat_total, 128), F32),
            pltpu.VMEM((np_, rows, lane_w), BF16),
            pltpu.VMEM((2, np_, rows, lane_w), BF16),
            pltpu.VMEM((lat_total // 128, 8 * degrees, 128), F32),
            pltpu.VMEM((per_x // 2 * degrees, lat_total), BF16),
            pltpu.VMEM((per_x // 2, lat_total, degrees), BF16),
            pltpu.VMEM((per_x * degrees, chans), F32),
            pltpu.VMEM((lane_w // 128, np_ * per_x, 128), F32),
            pltpu.VMEM((np_, per_x, lane_w), BF16),
            pltpu.VMEM((np_, per_x, lane_w), BF16),
            pltpu.VMEM((per_x * degrees, lane_w), F32),
            pltpu.VMEM((chans, 9 * chans), BF16),
            pltpu.VMEM((ch, 9 * chans), BF16),
            pltpu.VMEM((2 * lane_w, chans), BF16),
            pltpu.VMEM((lane_w, lane_w), BF16),
            pltpu.VMEM((degrees * ch, chans), BF16),
            pltpu.VMEM((2 * orders, width), BF16),
            pltpu.VMEM((2 * orders, width), BF16),
            pltpu.VMEM((rows, lane_w), F32),
            pltpu.VMEM((8, lat_total), F32),
            dma((5,)), dma((5,)), dma((2, np_)), dma((2, np_)), dma((np_,)), dma((np_,)), dma((5,)),
        ],
        compiler_params=pltpu.CompilerParams(
            collective_id=0, has_side_effects=True, vmem_limit_bytes=48 << 20
        ),
    )(x, w1, w2, cosine, mix, forward, inverse, quad, start)
    return out.reshape(ch, rows, width)


def solution(mesh):
    in_specs = (P("groups", "lat", "lon"), P(), P(), P(None, "lon", None))
    out_specs = P(("groups", "lon"), "lat", None)
    return jax.shard_map(
        functools.partial(local, mesh.shape["lat"]),
        mesh=mesh, in_specs=in_specs, out_specs=out_specs, check_vma=False,
    )
```

time: 29.9 us -> 32.9 us (1.10)
  local copies, waits for them, and re-layouts: 3.28 us -> 6.79 us
  Pallas kernels: 26.4 us -> 25.8 us
    unnamed x23 -> x18, local copies, waits for them, and re-layouts: 1 us -> 6.79 us
    transpose x3 -> x0, local copies, waits for them, and re-layouts: 1.97 us -> none  [the longest x1 1.08 us: local(): w2 = jnp.transpose(conv_second, (0, 2, 3, 1)).reshape(2, ch, 9 * chans)]
    pallas_call x1, Pallas kernels: 26.4 us -> 25.8 us  [local(): pl.pallas_call(functools.partial(body, (np_, rows, chans, half_w, degrees...]
where the time goes in v2:
time: 32.9 us; the launch traced here: 32.6 us
  Pallas kernels  25.8 us (78%)
  local copies, waits for them, and re-layouts  6.79 us (21%)
    pallas_call x1, Pallas kernels, local(): pl.pallas_call(functools.partial(body, (np_, rows, chans, half_w, degrees...  25.8 us
    unnamed x18, local copies, waits for them, and re-layouts  6.79 us

profile of v2, /device:TPU:0, one launch (start us, length us, event | category | flops | bytes accessed | tf_op | source)
XLA Modules:
  0.0 32.6 jit_solution(15130735210977226096)
XLA Ops:
  0.0 0.0 copy-start.1
  0.0 0.0 copy-start.4
  0.0 1.0 %copy.12 = bf16[64,8,128]{2,0,1:T(8,128)(2,1)S(1)} copy(bf16[64,8,128]{2,1,0:T(8,128)(2,1)} %param.9) | data formatting | bytes 262144 | tf_op args[0]
  1.0 0.0 copy-start.7
  1.0 0.0 copy-done.1
  1.0 0.0 copy-done.4
  1.0 0.6 %copy-done.7 = f32[1,128]{1,0:T(1,128)S(1)} copy-done((f32[1,128]{1,0:T(1,128)S(1)}, f32[1,128]{1,0:T(1,128)}, u32[]{:S(2)}) %copy-start.7) | copy-done | bytes 536
  1.6 0.0 copy-start
  1.6 1.0 %copy-done = bf16[64,32,64]{2,1,0:T(8,128)(2,1)S(1)} copy-done((bf16[64,32,64]{2,1,0:T(8,128)(2,1)S(1)}, bf16[64,32,64]{2,1,0:T(8,128)(2,1)}, u32[]{:S(2)}) %copy-start) | copy-done | bytes 262168
  2.7 0.0 copy-start.2
  2.7 0.9 %copy-done.2 = bf16[64,64,3,3]{1,0,3,2:T(8,128)(2,1)S(1)} copy-done((bf16[64,64,3,3]{1,0,3,2:T(8,128)(2,1)S(1)}, bf16[64,64,3,3]{1,0,3,2:T(8,128)(2,1)}, u32[]{:S(2)}) %copy-start.2) | copy-done | bytes 73752
  3.6 0.0 copy-start.3
  3.6 0.9 %copy-done.3 = f32[16,8,256]{2,1,0:T(8,128)S(1)} copy-done((f32[16,8,256]{2,1,0:T(8,128)S(1)}, f32[16,8,256]{2,1,0:T(8,128)}, u32[]{:S(2)}) %copy-start.3) | copy-done | bytes 131096
  4.5 0.0 copy-start.5
  4.5 0.8 %copy-done.5 = bf16[128,256]{1,0:T(8,128)(2,1)S(1)} copy-done((bf16[128,256]{1,0:T(8,128)(2,1)S(1)}, bf16[128,256]{1,0:T(8,128)(2,1)}, u32[]{:S(2)}) %copy-start.5) | copy-done | bytes 65560
  5.3 0.0 copy-start.6
  5.3 0.8 %copy-done.6 = bf16[128,256]{1,0:T(8,128)(2,1)S(1)} copy-done((bf16[128,256]{1,0:T(8,128)(2,1)S(1)}, bf16[128,256]{1,0:T(8,128)(2,1)}, u32[]{:S(2)}) %copy-start.6) | copy-done | bytes 65560
  6.2 25.8 %shard_map.91 = bf16[256,256]{1,0:T(8,128)(2,1)S(1)} custom-call(bf16[8,64,128]{2,1,0:T(8,128)(2,1)S(1)} %bitcast.9, bf16[3,3,64,64]{3,2,1,0:T(8,128)(2,1)S(1)} %bitcast.10, bf16[3,3,64,64]{3,2,1,0:T(8,128)(2,1)S(1)} %bitcast.11, f32[1,128]{1,0:T(1,128)S(1)} %copy-done.7, bf16[2048,64]{1,0:T(8,128)(2,1)S(1)} %bitcast.7, bf16[128,256]{1,0:T(8,128)(2,1)S(1)} %copy-done.6, ...), custom_call_target="tpu_custom_call" | custom-call | tf_op jit(solution)/shard_map/pallas_call | solution.py:380
  31.9 0.7 %copy.14 = bf16[32,8,256]{2,1,0:T(8,128)(2,1)} copy(bf16[32,8,256]{2,1,0:T(8,128)(2,1)S(1)} %bitcast.8) | data formatting | bytes 262144
Async XLA Ops:
  0.0 1.0 %copy-start.1 = (bf16[64,64,3,3]{1,0,3,2:T(8,128)(2,1)S(1)}, bf16[64,64,3,3]{1,0,3,2:T(8,128)(2,1)}, u32[]{:S(2)}) copy-start(bf16[64,64,3,3]{1,0,3,2:T(8,128)(2,1)} %param.10) | copy-start | bytes 221188
  0.0 1.0 %copy-start.4 = (f32[16,8,128]{2,1,0:T(8,128)S(1)}, f32[16,8,128]{2,1,0:T(8,128)}, u32[]{:S(2)}) copy-start(f32[16,8,128]{2,1,0:T(8,128)} %constant.14.clone.start_hbm) | copy-start | bytes 196612
  1.0 0.7 %copy-start.7 = (f32[1,128]{1,0:T(1,128)S(1)}, f32[1,128]{1,0:T(1,128)}, u32[]{:S(2)}) copy-start(f32[1,128]{1,0:T(1,128)} %constant.13.clone.cos_ref) | copy-start | bytes 1540
  1.6 1.0 %copy-start = (bf16[64,32,64]{2,1,0:T(8,128)(2,1)S(1)}, bf16[64,32,64]{2,1,0:T(8,128)(2,1)}, u32[]{:S(2)}) copy-start(bf16[64,32,64]{2,1,0:T(8,128)(2,1)} %param.12) | copy-start | bytes 786436
  2.7 0.9 %copy-start.2 = (bf16[64,64,3,3]{1,0,3,2:T(8,128)(2,1)S(1)}, bf16[64,64,3,3]{1,0,3,2:T(8,128)(2,1)}, u32[]{:S(2)}) copy-start(bf16[64,64,3,3]{1,0,3,2:T(8,128)(2,1)} %param.11) | copy-start | bytes 221188
  3.6 0.9 %copy-start.3 = (f32[16,8,256]{2,1,0:T(8,128)S(1)}, f32[16,8,256]{2,1,0:T(8,128)}, u32[]{:S(2)}) copy-start(f32[16,8,256]{2,1,0:T(8,128)} %constant.12.clone.quad_hbm) | copy-start | bytes 393220
  4.5 0.8 %copy-start.5 = (bf16[128,256]{1,0:T(8,128)(2,1)S(1)}, bf16[128,256]{1,0:T(8,128)(2,1)}, u32[]{:S(2)}) copy-start(bf16[128,256]{1,0:T(8,128)(2,1)} %constant.11.clone.inv_hbm) | copy-start | bytes 196612
  5.3 0.8 %copy-start.6 = (bf16[128,256]{1,0:T(8,128)(2,1)S(1)}, bf16[128,256]{1,0:T(8,128)(2,1)}, u32[]{:S(2)}) copy-start(bf16[128,256]{1,0:T(8,128)(2,1)} %constant.10.clone.fwd_hbm) | copy-start | bytes 196612

commit v3 on v2

--- a/solution.py
+++ b/solution.py
@@ -42,9 +42,10 @@
     start = (0.5 * np.log(ids + 0.5) + 0.5 * sums[ids])[:, None] + ids[:, None] * np.log(np.sin(theta[fold]))[None, :]
     start = start.reshape(lat_count, per_x // 2, lat_total)
     start = np.pad(start, ((0, 0), (0, 8 - per_x // 2), (0, 0)))
+    start[:, 7] = cosine
     as_bf = lambda a: jnp.asarray(np.asarray(a, np.float32).astype(jnp.bfloat16))
     as_f = lambda a: jnp.asarray(np.ascontiguousarray(a, np.float32))
-    return as_bf(forward), as_bf(inverse), as_f(quad), as_f(cosine), as_f(start)
+    return as_bf(forward), as_bf(inverse), as_f(quad), as_f(start)
 
 
 def peers(np_, me):
@@ -61,10 +62,10 @@
     return out
 
 
-def body(sizes, x_ref, w1_ref, w2_ref, cos_ref, mix_hbm, fwd_hbm, inv_hbm, quad_hbm, start_hbm, out_ref,
+def body(sizes, x_hbm, w1_hbm, w2_hbm, mix_hbm, fwd_hbm, inv_hbm, quad_hbm, start_hbm, out_ref,
          xin, slab1, slab2, hdup, tb, send_b, recv_b, lt, lt_b, lg, spec, tc, send_c, recv_c, mixed,
-         w1s, w2s, sq_s, sp_s, mix_s, fwd_s, inv_s, quad_s, start_s,
-         a_send, a_recv, b_send, b_recv, c_send, c_recv, l_sem):
+         x_s, x32, x_ref, w1_ref, w2_ref, w1s, w2s, sq_s, sp_s, mix_s, fwd_s, inv_s, quad_s, start_s,
+         a_send, a_recv, b_send, b_recv, c_send, c_recv, l_sem, ready):
     np_, rows, chans, half_w, degrees = sizes
     ch = chans // 2
     width = 2 * half_w
@@ -79,27 +80,62 @@
     barrier = pltpu.get_barrier_semaphore()
 
     others = peers(np_, me)
-    pl.semaphore_signal(barrier, inc=1, device_id={"lat": me, "lon": other}, device_id_type=MESH)
-    for p in others:
-        for h in (core, other):
-            pl.semaphore_signal(barrier, inc=1, device_id={"lat": p, "lon": h}, device_id_type=MESH)
+
+    def greet(p, h):
+        pl.semaphore_signal(barrier, inc=1, device_id={"lat": p, "lon": h}, device_id_type=MESH)
+
+    near = 1
+    while near * near < np_ or np_ % near:
+        near += 1
+    far = np_ // near
+    place = me % near
+    far_others = [(me + near * d) % np_ for d in range(1, far)]
+    crosses_up = (place == 0) & (me > 0)
+    crosses_down = (place == near - 1) & (me < np_ - 1)
+    for p in far_others:
+        greet(p, core)
+
+    @pl.when(crosses_up)
+    def _():
+        greet(me - 1, core)
+        greet(me - 1, other)
+
+    @pl.when(crosses_down)
+    def _():
+        greet(me + 1, core)
+        greet(me + 1, other)
+
+    for d in range(1, near):
+        p = me - place + (place + d) % near
+        greet(p, core)
+        greet(p, other)
+    greet(me, other)
 
     loads = [
         pltpu.make_async_copy(a, b, l_sem.at[k])
         for k, (a, b) in enumerate([
             (start_hbm.at[me], start_s), (quad_hbm.at[me], quad_s), (fwd_hbm, fwd_s),
-            (mix_hbm, mix_s), (inv_hbm, inv_s),
+            (mix_hbm, mix_s), (inv_hbm, inv_s), (x_hbm, x_s), (w1_hbm, w1_ref), (w2_hbm, w2_ref),
         ])
     ]
-    for load in loads:
-        load.start()
-
+    for k in (5, 6, 7, 0, 1, 2, 3, 4):
+        loads[k].start()
+
+    for k in (5, 6, 7):
+        loads[k].wait()
+    for v in range(half_w // 128):
+        x32[v] = x_s[:, :, v * 128 : (v + 1) * 128].astype(F32).reshape(chans * rows, 128)
+        for t in range(rows):
+            x_ref[t, :, v * 128 : (v + 1) * 128] = x32[v, pl.ds(t, chans, stride=rows), :].astype(BF16)
     for k in range(9):
         at = slice(k * chans, (k + 1) * chans)
         w1s[:, at] = w1_ref[k // 3, k % 3]
         w2s[:, at] = w2_ref[k // 3, k % 3, pl.ds(pl.multiple_of(core * ch, ch), ch), :]
 
-    pl.semaphore_wait(barrier, 2 * np_ - 1)
+    known = 2 * near - 1 + far - 1
+    pl.semaphore_wait(
+        barrier, known + 2 * crosses_up.astype(jnp.int32) + 2 * crosses_down.astype(jnp.int32)
+    )
 
     def across():
         return pltpu.make_async_remote_copy(
@@ -134,6 +170,9 @@
 
     across().start()
 
+    for p in far_others:
+        pl.semaphore_signal(ready, inc=1, device_id={"lat": p, "lon": core}, device_id_type=MESH)
+
     @pl.when(me == 0)
     def _():
         xin[:, pl.ds(0, 2)] = jnp.zeros((2, 2, chans, half_w), BF16)
@@ -145,7 +184,7 @@
     xin[core, pl.ds(2, rows)] = x_ref[...]
 
     loads[0].wait()
-    cosine = cos_ref[...]
+    cosine = start_s[7:8, :]
     log_start = start_s[...]
     wide_l = (8, degrees)
     order = (lax.broadcasted_iota(jnp.int32, wide_l, 0) + me * orders_here).astype(F32)
@@ -253,6 +292,8 @@
             [tb[xh, p * rows : (p + 1) * rows, :] for xh in range(lane_w // 128)], axis=1
         )
         send_b[p] = (piece * quad).astype(BF16)
+
+    pl.semaphore_wait(ready, far - 1)
 
     def b_copy(to_lat, to_core, from_lat, from_core):
         return pltpu.make_async_remote_copy(
@@ -369,18 +410,17 @@
     degrees = mixing.shape[0]
     per_x = 2 * orders // np_
     lane_w = per_x * ch
-    forward, inverse, quad, cosine, start = constant_tables(np_, rows, width, orders, lane_w)
-    x = jnp.transpose(fields, (1, 0, 2))
+    forward, inverse, quad, start = constant_tables(np_, rows, width, orders, lane_w)
     w1 = jnp.transpose(conv_first, (2, 3, 0, 1))
     w2 = jnp.transpose(conv_second, (2, 3, 0, 1))
     mix = mixing.reshape(degrees * ch, chans)
     vm = pl.BlockSpec(memory_space=pltpu.VMEM)
-    hbm = pl.BlockSpec(memory_space=pltpu.HBM)
+    hbm = pl.BlockSpec(memory_space=pl.ANY)
     dma = pltpu.SemaphoreType.DMA
     out = pl.pallas_call(
         functools.partial(body, (np_, rows, chans, half_w, degrees)),
         out_shape=jax.ShapeDtypeStruct((ch * rows, width), BF16),
-        in_specs=[vm] * 4 + [hbm] * 5,
+        in_specs=[hbm] * 8,
         out_specs=vm,
         scratch_shapes=[
             pltpu.VMEM((2, rows + 4, chans, half_w), BF16),
@@ -398,6 +438,11 @@
             pltpu.VMEM((np_, per_x, lane_w), BF16),
             pltpu.VMEM((np_, per_x, lane_w), BF16),
             pltpu.VMEM((per_x * degrees, lane_w), F32),
+            pltpu.VMEM((chans, rows, half_w), BF16),
+            pltpu.VMEM((half_w // 128, chans * rows, 128), F32),
+            pltpu.VMEM((rows, chans, half_w), BF16),
+            pltpu.VMEM((3, 3, chans, chans), BF16),
+            pltpu.VMEM((3, 3, chans, chans), BF16),
             pltpu.VMEM((chans, 9 * chans), BF16),
             pltpu.VMEM((ch, 9 * chans), BF16),
             pltpu.VMEM((2 * lane_w, chans), BF16),
@@ -407,12 +452,12 @@
             pltpu.VMEM((2 * orders, width), BF16),
             pltpu.VMEM((rows, lane_w), F32),
             pltpu.VMEM((8, lat_total), F32),
-            dma((5,)), dma((5,)), dma((2, np_)), dma((2, np_)), dma((np_,)), dma((np_,)), dma((5,)),
+            dma((5,)), dma((5,)), dma((2, np_)), dma((2, np_)), dma((np_,)), dma((np_,)), dma((8,)), pltpu.SemaphoreType.REGULAR,
         ],
         compiler_params=pltpu.CompilerParams(
-            collective_id=0, has_side_effects=True, vmem_limit_bytes=48 << 20
+            collective_id=0, has_side_effects=True, vmem_limit_bytes=60 << 20
         ),
-    )(x, w1, w2, cosine, mix, forward, inverse, quad, start)
+    )(fields, w1, w2, mix, forward, inverse, quad, start)
     return out.reshape(ch, rows, width)
 
 

time: 32.9 us -> 27 us (0.82)
  local copies, waits for them, and re-layouts: 6.79 us -> 1.57 us
  Pallas kernels: 25.8 us -> 25.2 us
    unnamed x18 -> x1, local copies, waits for them, and re-layouts: 6.79 us -> 1.57 us
    pallas_call x1, Pallas kernels: 25.8 us -> 25.2 us  [local(): pl.pallas_call(functools.partial(body, (np_, rows, chans, half_w, degrees...]
where the time goes in v3:
time: 27 us; the launch traced here: 26.8 us
  Pallas kernels  25.2 us (93%)
  local copies, waits for them, and re-layouts  1.57 us (6%)
    pallas_call x1, Pallas kernels, local(): pl.pallas_call(functools.partial(body, (np_, rows, chans, half_w, degrees...  25.2 us
    unnamed x1, local copies, waits for them, and re-layouts  1.57 us

profile of v3, /device:TPU:0, one launch (start us, length us, event | category | flops | bytes accessed | tf_op | source)
XLA Modules:
  0.0 26.8 jit_solution(10715973623192798275)
XLA Ops:
  0.0 25.2 %shard_map.82 = bf16[256,256]{1,0:T(8,128)(2,1)} custom-call(bf16[64,8,128]{2,1,0:T(8,128)(2,1)} %x_hbm.1, bf16[3,3,64,64]{3,2,1,0:T(8,128)(2,1)} %bitcast.6, bf16[3,3,64,64]{3,2,1,0:T(8,128)(2,1)} %bitcast.7, bf16[2048,64]{1,0:T(8,128)(2,1)} %bitcast.4, bf16[128,256]{1,0:T(8,128)(2,1)} %constant.8.clone.fwd_hbm, bf16[128,256]{1,0:T(8,128)(2,1)} %constant.9.clone.inv_hbm, ...), custom_call_target="tpu_custom_call" | custom-call | tf_op jit(solution)/shard_map/pallas_call | solution.py:420
  25.3 1.6 %copy.10 = bf16[32,8,256]{2,1,0:T(8,128)(2,1)} copy(bf16[32,8,256]{2,1,0:T(8,128)(2,1)} %bitcast.5) | data formatting | bytes 262144

commit v4 on v3

--- a/solution.py
+++ b/solution.py
@@ -303,9 +303,7 @@
         )
 
     for p in others:
-        for h in (core, other):
-            b_copy(p, h, me, core).start()
-    b_copy(me, other, me, core).start()
+        b_copy(p, core, me, core).start()
     recv_b[core, me] = send_b[me]
 
     for q in range(orders_here):
@@ -330,17 +328,26 @@
     loads[3].wait()
     loads[4].wait()
 
-    b_copy(me, other, me, other).wait_recv()
+    def pass_on(h):
+        return pltpu.make_async_remote_copy(
+            src_ref=recv_b.at[h], dst_ref=recv_b.at[h],
+            send_sem=b_send.at[other, 0], recv_sem=b_recv.at[h, 0],
+            device_id={"lat": me, "lon": other}, device_id_type=MESH,
+        )
+
     for q in reversed(others):
-        for h in (core, other):
-            b_copy(q, h, q, h).wait_recv()
+        b_copy(q, core, q, core).wait_recv()
+    pass_on(core).start()
 
     table = lt_b[...]
     x_lane = lax.broadcasted_iota(jnp.int32, (degrees, lane_w), 1) // ch
-    halves = []
-    for h in range(2):
-        r = recv_b[h].astype(F32).reshape(lat_total, lane_w).astype(BF16)
-        halves.append(mm(table, r))
+    def half(h):
+        return mm(table, recv_b[h].astype(F32).reshape(lat_total, lane_w).astype(BF16))
+
+    mine = half(core)
+    pass_on(other).wait_recv()
+    theirs = half(other)
+    halves = [jnp.where(core == 0, mine, theirs), jnp.where(core == 0, theirs, mine)]
     for x in range(per_x):
         q = x // 2
         part = [jnp.where(x_lane == x, u[q * degrees : (q + 1) * degrees, :], 0.0).astype(BF16) for u in halves]
@@ -388,10 +395,9 @@
         c_copy(p, me).start()
     recv_c[me] = send_c[me]
 
-    b_copy(me, other, me, core).wait_send()
+    pass_on(core).wait_send()
     for p in others:
-        for h in (core, other):
-            b_copy(p, h, me, core).wait_send()
+        b_copy(p, core, me, core).wait_send()
 
     for q in reversed(others):
         c_copy(q, q).wait_recv()

time: 27 us -> 25.9 us (0.959)
  Pallas kernels: 25.2 us -> 24.2 us
    pallas_call x1, Pallas kernels: 25.2 us -> 24.2 us  [local(): pl.pallas_call(functools.partial(body, (np_, rows, chans, half_w, degrees...]
where the time goes in v4:
time: 25.9 us; the launch traced here: 25.7 us
  Pallas kernels  24.2 us (93%)
  local copies, waits for them, and re-layouts  1.57 us (6%)
    pallas_call x1, Pallas kernels, local(): pl.pallas_call(functools.partial(body, (np_, rows, chans, half_w, degrees...  24.2 us
    unnamed x1, local copies, waits for them, and re-layouts  1.57 us

profile of v4, /device:TPU:0, one launch (start us, length us, event | category | flops | bytes accessed | tf_op | source)
XLA Modules:
  0.0 25.7 jit_solution(3295806782965527402)
XLA Ops:
  0.0 24.2 %shard_map.82 = bf16[256,256]{1,0:T(8,128)(2,1)} custom-call(bf16[64,8,128]{2,1,0:T(8,128)(2,1)} %x_hbm.1, bf16[3,3,64,64]{3,2,1,0:T(8,128)(2,1)} %bitcast.6, bf16[3,3,64,64]{3,2,1,0:T(8,128)(2,1)} %bitcast.7, bf16[2048,64]{1,0:T(8,128)(2,1)} %bitcast.4, bf16[128,256]{1,0:T(8,128)(2,1)} %constant.8.clone.fwd_hbm, bf16[128,256]{1,0:T(8,128)(2,1)} %constant.9.clone.inv_hbm, ...), custom_call_target="tpu_custom_call" | custom-call | tf_op jit(solution)/shard_map/pallas_call | solution.py:426
  24.2 1.6 %copy.10 = bf16[32,8,256]{2,1,0:T(8,128)(2,1)} copy(bf16[32,8,256]{2,1,0:T(8,128)(2,1)} %bitcast.5) | data formatting | bytes 262144
